TPU v7x, 256 devices: a whole 4x4x8 slice. The times are simulated.
256 devices in a mesh: kv: 8 (over y, z_hi), ex: 32 (over z_lo, x, core).
Axes of the slice: x: 4, y: 4, z: 8 (z_hi: 2, z_lo: 4; z = z_hi * 4 + z_lo), core: 2. Of those that a mesh axis runs over, the one named last changes fastest.
Arguments:
- x_tokens: bfloat16 [32, 576, 2048], P('ex'), may hold values from -6 to 6
- attn_gain: float32 [2048], replicated, may hold values from 0.1 to 1.9
- w_qkv: bfloat16 [2048, 3, 2048], P(None, None, 'kv'), may hold values from -1 to 1
- w_out: bfloat16 [2048, 2048], P('kv'), may hold values from -0.125 to 0.125
- cache: bfloat16 [64, 2, 512, 2048], P('ex', None, None, 'kv'), may hold values from -6 to 6
- cache_len: int32 [64], P('ex'), may hold values from 1 to 512, 16384 in all
- moe_gain: float32 [2048], replicated, may hold values from 0.1 to 1.9
- w_trainer: float32 [32, 3, 2048, 1024], P(None, None, 'ex', 'kv'), may hold values from -0.125 to 0.125
- expert_ids: int32 [32, 576, 8], P('ex', 'kv'), may hold values from 0 to 31, all different within a row; in each aligned block of 72 rows (0 to 71, 72 to 143, ..., all dimensions but the last counted through in order) at most 28 rows name the same one
- route_probs: float32 [32, 576, 8], P('ex', 'kv'), may hold values from 0.05 to 1
Outputs:
- layer_out: bfloat16 [32, 576, 2048], P('ex', 'kv')
Inputs may be any that keep to these rules, and one draw needn't show every extreme that they name: `expert_ids`: in each aligned block of 72 tokens, no expert is named by more than 28 of them; each token names 8 different experts.
All inputs are finite; a program needn't handle non-finite values. No bound on the sum of `cache_len` on one device may be relied on, other than what follows from the above.
Results may differ from a plain program's by a relative error of at most 0.0055.
Values may be sent and summed in bfloat16 or wider, within the bound.
A program may use at most 128 MiB of HBM per device.

v0:
```python
import math

import jax
import jax.numpy as jnp
from jax import lax
from jax.sharding import PartitionSpec as P

HD = 128
TOPK = 8
PLEN = 512
REQ_DEV = 2
QB = 32
CMAX = 512


def rms_scale(rows, gain):
    values = rows.astype(jnp.float32)
    scale = lax.rsqrt(jnp.mean(values * values, axis=-1, keepdims=True) + 1e-06)
    return values * scale * gain


def attend(query, keys, values, valid):
    scores = jnp.einsum(
        "qhd,khd->hqk", query, keys, preferred_element_type=jnp.float32
    ) / math.sqrt(HD)
    scores = jnp.where(valid[None, None, :], scores, -1e30)
    top = jnp.max(scores, axis=-1, keepdims=True)
    weights = jnp.exp(scores - top)
    probs = (weights / jnp.sum(weights, axis=-1, keepdims=True)).astype(jnp.bfloat16)
    mixed = jnp.einsum("hqk,khd->qhd", probs, values, preferred_element_type=jnp.float32)
    return mixed.astype(jnp.bfloat16)


def on_device(
    x_tokens,
    attn_gain,
    w_qkv,
    w_out,
    cache,
    cache_len,
    moe_gain,
    w_trainer,
    expert_ids,
    route_probs,
):
    trainer = w_trainer.astype(jnp.bfloat16)
    full_rows = lax.all_gather(trainer, "kv", axis=3, tiled=True)
    server = lax.all_to_all(full_rows, "ex", split_axis=0, concat_axis=2, tiled=True)
    rows = x_tokens[0]
    row_count = rows.shape[0]
    local_heads = w_qkv.shape[2] // HD
    normed = rms_scale(rows, attn_gain).astype(jnp.bfloat16)
    flat_qkv = w_qkv.reshape(w_qkv.shape[0], 3 * local_heads * HD)
    proj = jnp.dot(normed, flat_qkv, preferred_element_type=jnp.float32).astype(jnp.bfloat16)
    proj = proj.reshape(row_count, 3, local_heads, HD)
    query, keys, values = (proj[:, 0], proj[:, 1], proj[:, 2])
    prompt_out = attend(query[:PLEN], keys[:PLEN], values[:PLEN], jnp.ones((PLEN,), dtype=bool))
    req_q = query[PLEN:].reshape(REQ_DEV, QB, local_heads, HD)
    req_k = keys[PLEN:].reshape(REQ_DEV, QB, local_heads, HD)
    req_v = values[PLEN:].reshape(REQ_DEV, QB, local_heads, HD)
    all_k = jnp.concatenate([req_k, cache[:, 0].reshape(REQ_DEV, CMAX, local_heads, HD)], axis=1)
    all_v = jnp.concatenate([req_v, cache[:, 1].reshape(REQ_DEV, CMAX, local_heads, HD)], axis=1)
    live = jnp.arange(CMAX, dtype=jnp.int32)[None, :] < cache_len[:, None]
    valid = jnp.concatenate([jnp.ones((REQ_DEV, QB), dtype=bool), live], axis=1)
    req_out = jax.vmap(attend)(req_q, all_k, all_v, valid)
    heads_out = jnp.concatenate(
        [prompt_out, req_out.reshape(REQ_DEV * QB, local_heads, HD)], axis=0
    )
    heads_out = heads_out.reshape(row_count, local_heads * HD)
    rows_dev = row_count // lax.axis_size("kv")
    mixed = lax.psum_scatter(
        jnp.dot(heads_out, w_out, preferred_element_type=jnp.float32),
        "kv",
        scatter_dimension=0,
        tiled=True,
    )
    own_rows = lax.dynamic_slice_in_dim(rows, lax.axis_index("kv") * rows_dev, rows_dev, 0)
    resid = own_rows.astype(jnp.float32) + mixed
    moe_in = rms_scale(resid, moe_gain).astype(jnp.bfloat16)
    experts = w_trainer.shape[0]
    width = moe_in.shape[1]
    chosen = expert_ids[0]
    probs = route_probs[0]
    share = probs / jnp.sum(probs, axis=-1, keepdims=True)
    slot_cap = max(2, 8 * rows_dev * TOPK // (5 * experts))
    flat_ids = chosen.reshape(-1)
    onehot = (flat_ids[:, None] == jnp.arange(experts, dtype=jnp.int32)[None, :]).astype(jnp.int32)
    before = jnp.cumsum(onehot, axis=0) - onehot
    place = jnp.sum(before * onehot, axis=1)
    slot = flat_ids * slot_cap + place
    match = jnp.arange(experts * slot_cap, dtype=jnp.int32)[:, None] == slot[None, :]
    spread = jnp.sum(match.reshape(experts * slot_cap, rows_dev, TOPK).astype(jnp.float32), axis=-1)
    send = jnp.dot(spread.astype(jnp.bfloat16), moe_in, preferred_element_type=jnp.float32)
    send = send.astype(jnp.bfloat16).reshape(experts, slot_cap, width)
    block = lax.all_to_all(send, "ex", split_axis=0, concat_axis=0, tiled=True)
    sources = block.shape[0]
    slots = block.shape[1]
    flat_rows = block.reshape(sources * slots, width)
    gate = jnp.dot(flat_rows, server[0, 0], preferred_element_type=jnp.float32)
    up = jnp.dot(flat_rows, server[0, 1], preferred_element_type=jnp.float32)
    hidden = (jax.nn.silu(gate) * up).astype(jnp.bfloat16)
    result = lax.dot_general(
        hidden, server[0, 2], (((1,), (1,)), ((), ())), preferred_element_type=jnp.float32
    )
    result = result.astype(jnp.bfloat16).reshape(sources, slots, width)
    returned = lax.all_to_all(result, "ex", split_axis=0, concat_axis=0, tiled=True)
    table = returned.reshape(experts * slot_cap, width)
    picked = jnp.take(table, slot.reshape(rows_dev, TOPK), axis=0)
    moe_out = jnp.sum(share[:, :, None] * picked.astype(jnp.float32), axis=1)
    return (resid + moe_out).astype(jnp.bfloat16)[None]


def solution(mesh):
    return jax.shard_map(
        on_device,
        mesh=mesh,
        in_specs=(
            P("ex", None, None),
            P(),
            P(None, None, "kv"),
            P("kv", None),
            P("ex", None, None, "kv"),
            P("ex"),
            P(),
            P(None, None, "ex", "kv"),
            P("ex", "kv", None),
            P("ex", "kv", None),
        ),
        out_specs=P("ex", "kv", None),
        check_vma=False,
    )
```

profile of v0, /device:TPU:1, one launch (start us, length us, event | category | flops | bytes accessed | tf_op | source)
XLA Modules:
  0.0 922.6 jit_solution(5607438441511600187)
XLA Ops:
  6.5 2.3 fusion.2
  8.9 4.9 copy.87
  13.7 4.8 fusion.15
  18.6 2.9 reshape.179
  22.3 2.4 fusion.76
  24.8 2.3 fusion.75
  27.1 2.1 copy.120
  29.2 2.0 copy.100
  31.2 2.1 copy.122
  33.3 2.1 copy.95
  38.8 2.4 fusion.21
  42.1 3.3 fusion.83
  47.3 2.9 fusion.29
  50.4 3.4 convert_element_type.86
  56.8 131.6 %reduce-scatter.2.cloned.1.call-done = f32[72,2048]{1,0:T(8,128)} async-done(((f32[576,2048]{1,0:T(8,128)}), f32[72,2048]{1,0:T(8,128)}) %reduce-scatter.2.cloned.1.call-update) | async-done | bytes 589840 | tf_op jit(solution)/shard_map/reduce_scatter | solution.py:71
  189.7 4.1 convolution_convert_fusion
  193.8 5.8 reshape.185
  199.6 266.1 %all_to_all.28 = bf16[32,28,2048]{2,1,0:T(8,128)(2,1)} all-to-all(bf16[32,28,2048]{2,1,0:T(8,128)(2,1)} %reshape.185), channel_id=1, replica_groups=mesh['kv'=8,'ex'=32] {'ex'}, dimensions={0} | all-to-all | bytes 7340032 | tf_op jit(solution)/shard_map/all_to_all | solution.py:95
  465.7 16.5 %all-gather.2.cloned.1.call-done = bf16[32,3,64,1024]{3,2,1,0:T(8,128)(2,1)} async-done(((bf16[32,3,64,128]{3,2,1,0:T(8,128)(2,1)}), bf16[32,3,64,1024]{3,2,1,0:T(8,128)(2,1)}) %all-gather.2.cloned.1.call-update) | async-done | bytes 12582928 | tf_op jit(solution)/shard_map/all_gather | solution.py:47
  482.2 8.0 all-to-all-start.1
  490.1 5.8 reshape.186
  495.9 273.5 %all-to-all-done.1 = bf16[32,3,64,1024]{3,2,1,0:T(8,128)(2,1)} async-done(((bf16[32,3,64,1024]{3,2,1,0:T(8,128)(2,1)}), bf16[32,3,64,1024]{3,2,1,0:T(8,128)(2,1)}, u32[]{:S(2)}, u32[]{:S(2)}) %all-to-all-start.1) | async-done | bytes 12582944 | tf_op jit(solution)/shard_map/all_to_all | solution.py:48
  769.5 6.6 copy.111
  776.1 4.0 fusion.6
  780.1 4.4 multiply_convert_fusion
  784.6 5.5 fusion.8
  790.1 5.8 reshape.187
  795.9 7.1 all-to-all-start.2
  803.6 92.7 %all-to-all-done.2 = bf16[32,28,2048]{2,1,0:T(8,128)(2,1)} async-done(((bf16[32,28,2048]{2,1,0:T(8,128)(2,1)}), bf16[32,28,2048]{2,1,0:T(8,128)(2,1)}, u32[]{:S(2)}, u32[]{:S(2)}) %all-to-all-start.2) | async-done | bytes 3670048 | tf_op jit(solution)/shard_map/all_to_all | solution.py:106
  896.3 5.8 reshape.188
  902.2 8.9 gather_fusion
  911.1 2.7 multiply_reduce_fusion
  (62 shorter events, 14.1 us)
Async XLA Ops:
  6.5 40.8 %copy-start = (bf16[256,2048]{1,0:T(8,128)(2,1)S(1)}, bf16[256,2048]{1,0:T(8,128)(2,1)}, u32[]{:S(2)}) copy-start(bf16[256,2048]{1,0:T(8,128)(2,1)} %param.13) | copy-start | bytes 3145732
  6.5 181.9 %reduce-scatter.2.cloned.1.call-start = ((), (), s32[]{:S(2)}) async-start(), calls=%async_computation.4 | async-start | bytes 5308416 | tf_op jit(solution)/shard_map/reduce_scatter | solution.py:71
  8.8 4.9 copy-start.2
  8.8 4.9 copy-start.8
  13.7 11.0 %copy-start.7 = (s32[2]{0:T(128)S(1)}, s32[2]{0:T(128)}, u32[]{:S(2)}) copy-start(s32[2]{0:T(128)} %param.15) | copy-start | bytes 28
  50.3 3.5 copy-start.4
  50.3 139.4 %copy-start.6 = (f32[2048]{0:T(1024)S(1)}, f32[2048]{0:T(1024)}, u32[]{:S(2)}) copy-start(f32[2048]{0:T(1024)} %param.16) | copy-start | bytes 24580
  50.3 431.9 %all-gather.2.cloned.1.call-start = ((), (), s32[]{:S(2)}) async-start(), calls=%async_computation.5 | async-start | bytes 14155776 | tf_op jit(solution)/shard_map/all_gather | solution.py:47
  482.2 287.3 %all-to-all-start.1 = ((bf16[32,3,64,1024]{3,2,1,0:T(8,128)(2,1)}), bf16[32,3,64,1024]{3,2,1,0:T(8,128)(2,1)}, u32[]{:S(2)}, u32[]{:S(2)}) async-start(bf16[32,3,64,1024]{3,2,1,0:T(8,128)(2,1)} %all-gather.2.cloned.1.call-done), calls=%async_computation.2 | async-start | bytes 25165824 | tf_op jit(solution)/shard_map/all_to_all | solution.py:48
  769.5 6.6 copy-start.3
  795.9 7.2 copy-start.5
  795.9 100.4 %all-to-all-start.2 = ((bf16[32,28,2048]{2,1,0:T(8,128)(2,1)}), bf16[32,28,2048]{2,1,0:T(8,128)(2,1)}, u32[]{:S(2)}, u32[]{:S(2)}) async-start(bf16[32,28,2048]{2,1,0:T(8,128)(2,1)} %reshape.187), calls=%async_computation.3 | async-start | bytes 8388608 | tf_op jit(solution)/shard_map/all_to_all | solution.py:106
  902.2 13.6 %copy-start.1 = (bf16[256,2048]{1,0:T(8,128)(2,1)S(1)}, bf16[256,2048]{1,0:T(8,128)(2,1)}, u32[]{:S(2)}) copy-start(bf16[256,2048]{1,0:T(8,128)(2,1)} %param.13) | copy-start | bytes 3145732
Sparse Core Ops, SparseCore 0:
  50.4 138.0 reduce-scatter.1
  191.2 290.8 all-gather.1
where the time goes:
time: 924 us; the launch traced here: 923 us
  waiting for transfers between devices  514 us (56%)
  blocking collectives  266 us (29%)
  local copies, waits for them, and re-layouts  64.3 us (7%)
  matrix products  34.9 us (4%)
  starting transfers between devices  15.1 us (2%)
  other arithmetic  14.1 us (2%)
  between operations  13.7 us (1%)
    all_to_all x1, waiting for transfers between devices, on_device(): lax.all_to_all(full_rows, 'ex', split_axis=0, concat_axis=2, tiled=True)  274 us
    all_to_all x1, blocking collectives, on_device(): block = lax.all_to_all(send, 'ex', split_axis=0, concat_axis=0, tiled=True)  266 us
    reduce_scatter x1, waiting for transfers between devices, on_device(): lax.psum_scatter(jnp.dot(heads_out, w_out, preferred_element_type=jnp.flo...  132 us
    all_to_all x1, waiting for transfers between devices, on_device(): lax.all_to_all(result, 'ex', split_axis=0, concat_axis=0, tiled=True)  92.7 us
  transfers between devices with their start and end apart: 4, of which 4 were waited for; matrix products, arithmetic and copies ran while one was open for 3% of the time, Pallas kernels for 0%

commit v1 on v0

--- a/solution.py
+++ b/solution.py
@@ -3,6 +3,8 @@
 import jax
 import jax.numpy as jnp
 from jax import lax
+from jax.experimental import pallas as pl
+from jax.experimental.pallas import tpu as pltpu
 from jax.sharding import PartitionSpec as P
 
 HD = 128
@@ -11,6 +13,133 @@
 REQ_DEV = 2
 QB = 32
 CMAX = 512
+
+
+MESH = pl.DeviceIdType.MESH
+
+
+def position():
+    kv, ex = lax.axis_index("kv"), lax.axis_index("ex")
+    return (ex // 2) % 4, kv // 2, (kv % 2) * 4 + ex // 8, ex % 2
+
+
+def device(x, y, z, c):
+    x, y, z, c = (x + 8) % 4, (y + 8) % 4, (z + 16) % 8, c % 2
+    return y * 2 + z // 4, ((z % 4) * 4 + x) * 2 + c
+
+
+def same_y(k):
+    return [(dx, k, dc) for dx in (1, 3, 2, 0) for dc in (0, 1)]
+
+
+def weights_kernel(own_ref, out_ref, send_sem, recv_sem, ysend_sem, yrecv_sem):
+    x, y, z, c = position()
+    kv, ex = device(x, y, z, c)
+    rows = own_ref.shape[2]
+    barrier = pltpu.get_barrier_semaphore()
+
+    @pl.loop(0, 8)
+    def _(k):
+        for dx in range(4):
+            for dc in range(2):
+                if dx or dc:
+                    pl.semaphore_signal(
+                        barrier, inc=1, device_id=device(x + dx, y, z + k, c + dc), device_id_type=MESH
+                    )
+
+    @pl.loop(1, 8)
+    def _(k):
+        pl.semaphore_signal(barrier, inc=1, device_id=device(x, y, z + k, c), device_id_type=MESH)
+
+    for dy in (1, 2, 3):
+        pl.semaphore_signal(barrier, inc=1, device_id=device(x, y + dy, z, c), device_id_type=MESH)
+    pl.semaphore_wait(barrier, 66)
+
+    def piece(k, dx, dc):
+        dz = (3 * k) % 8
+        to = device(x + dx, y, z + dz, c + dc)
+        return pltpu.make_async_remote_copy(
+            src_ref=own_ref.at[to[1]],
+            dst_ref=out_ref.at[kv, :, pl.ds(pl.multiple_of(ex * rows, rows), rows), :],
+            send_sem=send_sem.at[k],
+            recv_sem=recv_sem.at[k],
+            device_id=to,
+            device_id_type=MESH,
+        )
+
+    local = pltpu.make_async_copy(
+        own_ref.at[ex],
+        out_ref.at[kv, :, pl.ds(pl.multiple_of(ex * rows, rows), rows), :],
+        recv_sem.at[0],
+    )
+    local.start()
+    for dx in (1, 3, 2, 0):
+        for dc in (0, 1):
+            if dx or dc:
+                piece(0, dx, dc).start()
+
+    @pl.loop(1, 8)
+    def _(k):
+        for dx in (1, 3, 2, 0):
+            for dc in (0, 1):
+                piece(k, dx, dc).start()
+
+    whole = 8 * rows
+
+    def group(k):
+        dz = (3 * k) % 8
+        zs = (z + 8 - dz) % 8
+        first = pl.multiple_of((zs % 4) * whole, whole)
+        return out_ref.at[y * 2 + zs // 4, :, pl.ds(first, whole), :]
+
+    def spread(k, dy):
+        return pltpu.make_async_remote_copy(
+            src_ref=group(k),
+            dst_ref=group(k),
+            send_sem=ysend_sem.at[dy, k],
+            recv_sem=yrecv_sem.at[dy, k],
+            device_id=device(x, y + dy, z, c),
+            device_id_type=MESH,
+        )
+
+    @pl.loop(0, 8)
+    def _(k):
+        pltpu.make_async_copy(group(k), group(k), recv_sem.at[k]).wait()
+        for dy in (1, 3, 2):
+            spread(k, dy).start()
+
+    def sent(k, count):
+        part = own_ref.at[pl.ds(0, count)]
+        pltpu.make_async_copy(part, part, send_sem.at[k]).wait()
+
+    sent(0, 7)
+
+    @pl.loop(1, 8)
+    def _(k):
+        sent(k, 8)
+
+    @pl.loop(0, 8)
+    def _(k):
+        for dy in (1, 2, 3):
+            spread(k, dy).wait()
+
+
+def gather_weights(own):
+    experts, three, rows, cols = own.shape
+    return pl.pallas_call(
+        weights_kernel,
+        out_shape=jax.ShapeDtypeStruct((8, three, 32 * rows, cols), own.dtype),
+        in_specs=[pl.BlockSpec(memory_space=pltpu.VMEM)],
+        out_specs=pl.BlockSpec(memory_space=pl.ANY),
+        scratch_shapes=[
+            pltpu.SemaphoreType.DMA((8,)),
+            pltpu.SemaphoreType.DMA((8,)),
+            pltpu.SemaphoreType.DMA((4, 8)),
+            pltpu.SemaphoreType.DMA((4, 8)),
+        ],
+        compiler_params=pltpu.CompilerParams(collective_id=0, has_side_effects=True),
+        name="gather_weights",
+    )(own)
 
 
 def rms_scale(rows, gain):
@@ -44,8 +173,8 @@
     route_probs,
 ):
     trainer = w_trainer.astype(jnp.bfloat16)
-    full_rows = lax.all_gather(trainer, "kv", axis=3, tiled=True)
-    server = lax.all_to_all(full_rows, "ex", split_axis=0, concat_axis=2, tiled=True)
+    whole = gather_weights(trainer)
+    server = whole.transpose(1, 2, 0, 3).reshape(1, 3, x_tokens.shape[2], -1)
     rows = x_tokens[0]
     row_count = rows.shape[0]
     local_heads = w_qkv.shape[2] // HD

time: 924 us -> 648 us (0.70)
  waiting for transfers between devices: 514 us -> 227 us
  Pallas kernels: 0 us -> 266 us
  blocking collectives: 266 us -> 0 us
  local copies, waits for them, and re-layouts: 64.3 us -> 75.9 us
    all_to_all x1, waiting for transfers between devices: 274 us -> 0.01 us  [on_device(): block = lax.all_to_all(send, 'ex', split_axis=0, concat_axis=0, tiled=True)]
    all_to_all x1 -> x0, blocking collectives: 266 us -> none  [on_device(): block = lax.all_to_all(send, 'ex', split_axis=0, concat_axis=0, tiled=True)]
    pallas_call x0 -> x1, Pallas kernels: none -> 266 us  [gather_weights(): pl.pallas_call(weights_kernel, out_shape=jax.ShapeDtypeStruct((8, three,...]
    transpose x0 -> x1, local copies, waits for them, and re-layouts: none -> 16.7 us  [on_device(): server = whole.transpose(1, 2, 0, 3).reshape(1, 3, x_tokens.shape[2], -1)]
    all_gather x1 -> x0, waiting for transfers between devices: 16.5 us -> none  [on_device(): full_rows = lax.all_gather(trainer, 'kv', axis=3, tiled=True)]
  transfers between devices with their start and end apart: 4 -> 3, of which waited for: 4 -> 2; matrix products, arithmetic and copies ran while one was open for 3% -> 4% of each run, Pallas kernels for 0% -> 41%
where the time goes in v1:
time: 648 us; the launch traced here: 646 us
  Pallas kernels  266 us (41%)
  waiting for transfers between devices  227 us (35%)
  local copies, waits for them, and re-layouts  75.9 us (12%)
  matrix products  37.9 us (6%)
  between operations  13.6 us (2%)
  starting transfers between devices  13.3 us (2%)
  other arithmetic  12.3 us (2%)
    pallas_call x1, Pallas kernels, gather_weights(): pl.pallas_call(weights_kernel, out_shape=jax.ShapeDtypeStruct((8, three,...  266 us
    reduce_scatter x1, waiting for transfers between devices, on_device(): lax.psum_scatter(jnp.dot(heads_out, w_out, preferred_element_type=jnp.flo...  135 us
    all_to_all x1, waiting for transfers between devices, on_device(): lax.all_to_all(result, 'ex', split_axis=0, concat_axis=0, tiled=True)  92.7 us
    transpose x1, local copies, waits for them, and re-layouts, on_device(): server = whole.transpose(1, 2, 0, 3).reshape(1, 3, x_tokens.shape[2], -1)  16.7 us
  transfers between devices with their start and end apart: 3, of which 2 were waited for; matrix products, arithmetic and copies ran while one was open for 4% of the time, Pallas kernels for 41%

profile of v1, /device:TPU:1, one launch (start us, length us, event | category | flops | bytes accessed | tf_op | source)
XLA Modules:
  0.0 646.1 jit_solution(15993409841354373373)
XLA Ops:
  6.5 4.9 copy.64
  12.0 4.8 fusion.15
  16.8 2.9 reshape.182
  20.5 2.4 fusion.76
  23.0 2.3 fusion.75
  25.3 2.1 copy.97
  27.3 2.0 copy.77
  29.5 2.1 copy.99
  31.5 2.1 copy.72
  35.2 2.4 fusion.21
  38.5 1.8 copy.92
  40.3 3.2 fusion.83
  43.5 2.0 convolution_convert_fusion.1
  45.6 2.9 fusion.29
  52.2 134.6 %reduce-scatter.2.cloned.1.call-done = f32[72,2048]{1,0:T(8,128)} async-done(((f32[576,2048]{1,0:T(8,128)}), f32[72,2048]{1,0:T(8,128)}) %reduce-scatter.2.cloned.1.call-update) | async-done | bytes 589840 | tf_op jit(solution)/shard_map/reduce_scatter | solution.py:200
  188.1 4.1 convolution_convert_fusion
  192.2 5.8 reshape.188
  198.0 6.4 all-to-all-start
  204.4 3.4 convert_element_type.86.own_ref
  207.8 265.7 %gather_weights.1 = bf16[8,3,2048,128]{3,2,1,0:T(8,128)(2,1)} custom-call(bf16[32,3,64,128]{3,2,1,0:T(8,128)(2,1)} %convert_element_type.86.own_ref), custom_call_target="tpu_custom_call" | custom-call | tf_op jit(solution)/shard_map/gather_weights/pallas_call | solution.py:129
  473.5 16.7 %copy.88 = bf16[3,2048,8,128]{1,3,2,0:T(8,128)(2,1)} copy(bf16[3,2048,8,128]{3,1,0,2:T(8,128)(2,1)} %bitcast.107) | data formatting | bytes 25165824 | tf_op jit(solution)/shard_map/transpose | solution.py:177
  490.2 5.8 reshape.189
  496.0 7.1 %fusion.6 = f32[896,1024]{1,0:T(8,128)S(1)} fusion(bf16[896,2048]{1,0:T(8,128)(2,1)} %reshape.189, bf16[1,3,2048,1024]{2,3,1,0:T(8,128)(2,1)} %bitcast.108), kind=kOutput, calls=%fused_computation.12 | convolution fusion | flops 3758096384 | bytes 11534336 | tf_op jit(solution)/shard_map/dot_general | solution.py:229
  504.0 4.5 multiply_convert_fusion
  508.4 5.4 fusion.8
  513.9 5.8 reshape.191
  519.7 6.8 %all-to-all-start.1 = ((bf16[32,28,2048]{2,1,0:T(8,128)(2,1)}), bf16[32,28,2048]{2,1,0:T(8,128)(2,1)}, u32[]{:S(2)}, u32[]{:S(2)}) async-start(bf16[32,28,2048]{2,1,0:T(8,128)(2,1)} %reshape.191), calls=%async_computation.2 | async-start | bytes 8388608 | tf_op jit(solution)/shard_map/all_to_all | solution.py:235
  527.1 92.7 %all-to-all-done.1 = bf16[32,28,2048]{2,1,0:T(8,128)(2,1)} async-done(((bf16[32,28,2048]{2,1,0:T(8,128)(2,1)}), bf16[32,28,2048]{2,1,0:T(8,128)(2,1)}, u32[]{:S(2)}, u32[]{:S(2)}) %all-to-all-start.1) | async-done | bytes 3670048 | tf_op jit(solution)/shard_map/all_to_all | solution.py:235
  619.9 5.8 reshape.192
  625.7 8.9 %gather_fusion = bf16[576,2048]{1,0:T(8,128)(2,1)S(1)} fusion(bf16[896,2048]{1,0:T(8,128)(2,1)} %reshape.192, s32[1024]{0:T(1024)S(1)} %pad_clamp_fusion), kind=kCustom, calls=%fused_computation | custom fusion | bytes 4720896 | tf_op jit(solution)/shard_map/jit(_take)/gather | solution.py:237
  634.6 2.7 multiply_reduce_fusion
  637.3 2.0 fusion.33
  (61 shorter events, 10.3 us)
Async XLA Ops:
  6.5 39.0 %copy-start = (bf16[256,2048]{1,0:T(8,128)(2,1)S(1)}, bf16[256,2048]{1,0:T(8,128)(2,1)}, u32[]{:S(2)}) copy-start(bf16[256,2048]{1,0:T(8,128)(2,1)} %param.13) | copy-start | bytes 3145732
  6.5 4.9 copy-start.3
  6.5 5.4 copy-start.9
  6.5 180.3 %reduce-scatter.2.cloned.1.call-start = ((), (), s32[]{:S(2)}) async-start(), calls=%async_computation.3 | async-start | bytes 5308416 | tf_op jit(solution)/shard_map/reduce_scatter | solution.py:200
  16.8 12.6 %copy-start.8 = (s32[2]{0:T(128)S(1)}, s32[2]{0:T(128)}, u32[]{:S(2)}) copy-start(s32[2]{0:T(128)} %param.15) | copy-start | bytes 28
  48.5 0.7 copy-start.5
  48.5 139.6 %copy-start.7 = (f32[2048]{0:T(1024)S(1)}, f32[2048]{0:T(1024)}, u32[]{:S(2)}) copy-start(f32[2048]{0:T(1024)} %param.16) | copy-start | bytes 24580
  198.0 292.3 %all-to-all-start = ((bf16[32,28,2048]{2,1,0:T(8,128)(2,1)}), bf16[32,28,2048]{2,1,0:T(8,128)(2,1)}, u32[]{:S(2)}, u32[]{:S(2)}) async-start(bf16[32,28,2048]{2,1,0:T(8,128)(2,1)} %reshape.188), calls=%async_computation.1 | async-start | bytes 8388608 | tf_op jit(solution)/shard_map/all_to_all | solution.py:224
  496.0 7.1 %copy-start.2 = (bf16[3,2048,8,128]{1,3,2,0:T(8,128)(2,1)S(1)}, bf16[3,2048,8,128]{1,3,2,0:T(8,128)(2,1)}, u32[]{:S(2)}) copy-start(bf16[3,2048,8,128]{1,3,2,0:T(8,128)(2,1)} %copy.88) | copy-start | bytes 37748740
  496.0 7.9 %copy-start.4 = (bf16[896,2048]{1,0:T(8,128)(2,1)S(1)}, bf16[896,2048]{1,0:T(8,128)(2,1)}, u32[]{:S(2)}) copy-start(bf16[896,2048]{1,0:T(8,128)(2,1)} %reshape.189) | copy-start | bytes 11010052
  519.7 7.3 %copy-start.6 = (f32[1,72,8]{1,2,0:T(8,128)S(1)}, f32[1,72,8]{1,2,0:T(8,128)}, u32[]{:S(2)}) copy-start(f32[1,72,8]{1,2,0:T(8,128)} %param.19) | copy-start | bytes 6916
  519.7 100.2 %all-to-all-start.1 = ((bf16[32,28,2048]{2,1,0:T(8,128)(2,1)}), bf16[32,28,2048]{2,1,0:T(8,128)(2,1)}, u32[]{:S(2)}, u32[]{:S(2)}) async-start(bf16[32,28,2048]{2,1,0:T(8,128)(2,1)} %reshape.191), calls=%async_computation.2 | async-start | bytes 8388608 | tf_op jit(solution)/shard_map/all_to_all | solution.py:235
  625.7 13.6 %copy-start.1 = (bf16[256,2048]{1,0:T(8,128)(2,1)S(1)}, bf16[256,2048]{1,0:T(8,128)(2,1)}, u32[]{:S(2)}) copy-start(bf16[256,2048]{1,0:T(8,128)(2,1)} %param.13) | copy-start | bytes 3145732
Sparse Core Ops, SparseCore 0:
  48.6 138.1 reduce-scatter.1

commit v2 on v0

v2 whole, which is shorter than its diff:
```python
import math

import jax
import jax.numpy as jnp
from jax import lax
from jax.experimental import pallas as pl
from jax.experimental.pallas import tpu as pltpu
from jax.sharding import PartitionSpec as P

HD = 128
TOPK = 8
PLEN = 512
REQ_DEV = 2
QB = 32
CMAX = 512
EXPERTS = 32
CAP = 28
WIDTH = 2048
ROWS = 576
OWN = 72
PAIR = 2 * CAP
SLOTS = 8 * PAIR
WIDE = 512
MESH = pl.DeviceIdType.MESH
F32 = jnp.float32
BF16 = jnp.bfloat16


def position():
    kv, ex = lax.axis_index("kv"), lax.axis_index("ex")
    return (ex // 2) % 4, kv // 2, (kv % 2) * 4 + ex // 8, ex % 2


def device(x, y, z, c):
    x, y, z, c = (x + 8) % 4, (y + 8) % 4, (z + 16) % 8, c % 2
    return y * 2 + z // 4, ((z % 4) * 4 + x) * 2 + c


def send_to(src, dst, send_sem, recv_sem, to):
    return pltpu.make_async_remote_copy(
        src_ref=src, dst_ref=dst, send_sem=send_sem, recv_sem=recv_sem, device_id=to, device_id_type=MESH
    )


def wait_bytes(ref, sem):
    pltpu.make_async_copy(ref, ref, sem).wait()


def times(a, b, contract=((1,), (0,))):
    return lax.dot_general(a, b, (contract, ((), ())), preferred_element_type=F32)


def softmax(parts):
    top = parts[0].max(axis=-1, keepdims=True)
    for part in parts[1:]:
        top = jnp.maximum(top, part.max(axis=-1, keepdims=True))
    parts = [jnp.exp(part - top) for part in parts]
    total = parts[0].sum(axis=-1, keepdims=True)
    for part in parts[1:]:
        total = total + part.sum(axis=-1, keepdims=True)
    return [(part / total).astype(BF16) for part in parts]


def layer_kernel(
    own_w, x_ref, own_x, attn_gain, w_qkv, w_out, cache, bias, moe_gain, route,
    out_ref,
    wbuf, proj, heads, part, y_out, y_in, z_out, z_in, resid, ztok, zroute, packs, slots, total, rback, c_out, c_in,
    a_send, a_recv, s_send, s_recv, r_send, r_recv, y_send, y_recv, z_send, z_recv,
    t_send, t_recv, m_send, m_recv, p_send, p_recv, b_send, b_recv, c_send, c_recv,
):
    x, y, z, c = position()
    kv, ex = device(x, y, z, c)
    zl, zh = z % 4, z // 4
    piece_rows = own_w.shape[2]
    barrier = pltpu.get_barrier_semaphore()

    @pl.loop(0, 8)
    def _(k):
        for dx in range(4):
            for dc in range(2):
                if dx or dc:
                    pl.semaphore_signal(
                        barrier, inc=1, device_id=device(x + dx, y, z + k, c + dc), device_id_type=MESH
                    )

    @pl.loop(1, 8)
    def _(k):
        pl.semaphore_signal(barrier, inc=1, device_id=device(x, y, z + k, c), device_id_type=MESH)

    for dy in (1, 2, 3):
        pl.semaphore_signal(barrier, inc=1, device_id=device(x, y + dy, z, c), device_id_type=MESH)
    pl.semaphore_wait(barrier, 66)

    def route_copy(r):
        return send_to(
            route.at[(zl + r) % 4], zroute.at[zl], m_send.at[r], m_recv.at[r],
            device(x, y, zh * 4 + (zl + r) % 4, c),
        )

    for r in (1, 2, 3):
        route_copy(r).start()
    own_route = pltpu.make_async_copy(route.at[zl], zroute.at[zl], m_recv.at[0])
    own_route.start()

    own_rows = pl.ds(pl.multiple_of(ex * piece_rows, piece_rows), piece_rows)

    def piece(k, dx, dc):
        to = device(x + dx, y, z + (3 * k) % 8, c + dc)
        return send_to(own_w.at[to[1]], wbuf.at[kv, :, own_rows, :], a_send.at[k], a_recv.at[k], to)

    pltpu.make_async_copy(own_w.at[ex], wbuf.at[kv, :, own_rows, :], a_recv.at[0]).start()
    for dx in (1, 3, 2, 0):
        for dc in (0, 1):
            if dx or dc:
                piece(0, dx, dc).start()

    @pl.loop(1, 8)
    def _(k):
        for dx in (1, 3, 2, 0):
            for dc in (0, 1):
                piece(k, dx, dc).start()

    whole = 8 * piece_rows

    def group(k, dy, first=0, count=whole):
        zs = (z + 8 - (3 * k) % 8) % 8
        begin = pl.multiple_of((zs % 4) * whole + first, piece_rows)
        return wbuf.at[((y + dy) % 4) * 2 + zs // 4, :, pl.ds(begin, count), :]

    half = whole // 2

    def spread(k):
        wait_bytes(group(k, 0), a_recv.at[k])
        for way, dy in ((0, 1), (1, 3)):
            send_to(
                group(k, 0), group(k, 0), s_send.at[way, k], s_recv.at[way, k], device(x, y + dy, z, c)
            ).start()

    def relay(k):
        for way, dy in ((0, 1), (1, 3)):
            wait_bytes(group(k, 4 - dy), s_recv.at[way, k])
            passed = group(k, 4 - dy, way * half, half)
            send_to(passed, passed, r_send.at[way, k], r_recv.at[way, k], device(x, y + dy, z, c)).start()

    @pl.loop(0, 2)
    def _(i):
        rows = pl.ds(pl.multiple_of(i * (ROWS // 2), ROWS // 2), ROWS // 2)
        values = x_ref[rows, :].astype(F32)
        scale = lax.rsqrt(jnp.mean(values * values, axis=-1, keepdims=True) + 1e-06)
        normed = (values * scale * attn_gain[...]).astype(BF16)
        proj[rows, :] = times(normed, w_qkv[...]).astype(BF16)

    spread(0)

    def lanes(which, head):
        return pl.ds((which * 2 + head) * HD, HD)

    inv = 1.0 / math.sqrt(HD)
    tile = 128
    for head in range(2):
        @pl.loop(0, PLEN // tile)
        def _(i):
            rows = pl.ds(pl.multiple_of(i * tile, tile), tile)
            scores = times(proj[rows, lanes(0, head)], proj[0:PLEN, lanes(1, head)], ((1,), (1,))) * inv
            (probs,) = softmax([scores])
            heads[rows, pl.ds(head * HD, HD)] = times(probs, proj[0:PLEN, lanes(2, head)]).astype(BF16)

        for req in range(REQ_DEV):
            rows = pl.ds(PLEN + req * QB, QB)
            query = proj[rows, lanes(0, head)]
            near = times(query, proj[rows, lanes(1, head)], ((1,), (1,))) * inv
            far = times(query, cache[req, 0, :, pl.ds(head * HD, HD)], ((1,), (1,))) * inv
            far = far + bias[req:req + 1, :]
            near, far = softmax([near, far])
            mixed = times(near, proj[rows, lanes(2, head)]) + times(far, cache[req, 1, :, pl.ds(head * HD, HD)])
            heads[rows, pl.ds(head * HD, HD)] = mixed.astype(BF16)
        spread(1 + head)

    quarter = ROWS // 4

    def block(dy):
        return heads[pl.ds(pl.multiple_of(((y + dy) % 4) * quarter, quarter), quarter), :]

    def y_copy(dy):
        return send_to(y_out.at[dy], y_in.at[dy], y_send.at[dy], y_recv.at[dy], device(x, y + dy, z, c))

    for dy in (2, 1, 3):
        y_out[dy] = times(block(dy), w_out[...]).astype(BF16)
        y_copy(dy).start()
    part[...] = times(block(0), w_out[...])
    spread(3)
    relay(0)
    for dy in (1, 3, 2):
        y_copy(dy).wait_recv()
        part[...] += y_in[dy].astype(F32)
    z_out[...] = part[pl.ds(pl.multiple_of((1 - zh) * OWN, OWN), OWN), :].astype(BF16)
    z_copy = send_to(z_out, z_in, z_send, z_recv, device(x, y, z + 4, c))
    z_copy.start()
    spread(4)
    relay(1)
    z_copy.wait_recv()
    sums = part[pl.ds(pl.multiple_of(zh * OWN, OWN), OWN), :] + z_in[...].astype(F32)
    sums = own_x[...].astype(F32) + sums
    resid[...] = sums
    scale = lax.rsqrt(jnp.mean(sums * sums, axis=-1, keepdims=True) + 1e-06)
    ztok[zl] = (sums * scale * moe_gain[...]).astype(BF16)

    def token_copy(r):
        return send_to(
            ztok.at[zl], ztok.at[zl], t_send.at[r], t_recv.at[r], device(x, y, zh * 4 + (zl + r) % 4, c)
        )

    for r in (1, 3, 2):
        token_copy(r).start()
    own_route.wait()
    for r in (1, 2, 3):
        wait_bytes(zroute.at[0], m_recv.at[r])

    def source(pair, b):
        return ((zl // 2 + pair) % 2) * 2 + b

    def spots(b, lane_axis):
        shape = (OWN, SLOTS) if lane_axis else (SLOTS, OWN)
        spot = lax.broadcasted_iota(jnp.int32, shape, 1 if lane_axis else 0) % PAIR
        return (spot - b * CAP).astype(F32)

    def picker(which, lane_axis):
        shape = (128, SLOTS) if lane_axis else (SLOTS, 128)
        expert = lax.broadcasted_iota(jnp.int32, shape, 1 if lane_axis else 0) // PAIR
        field = lax.broadcasted_iota(jnp.int32, shape, 0 if lane_axis else 1)
        return (field == expert + which * 8).astype(F32).astype(BF16)

    def packet(pair, dx, dc):
        to = device(x + dx, y, z, c + dc)
        return send_to(
            packs.at[pair, ((x + dx) % 4) * 2 + (c + dc) % 2], slots.at[pair, x * 2 + c],
            p_send.at[pair], p_recv.at[pair], to,
        )

    def pack(pair):
        hits = []
        for b in range(2):
            place = times(picker(0, False), zroute[source(pair, b)], ((1,), (1,)))
            hits.append(jnp.where(place == spots(b, False), 1.0, 0.0).astype(BF16))
        for n in range(0, WIDTH, WIDE):
            cols = pl.ds(n, WIDE)
            rows = times(hits[0], ztok[source(pair, 0), :, cols]) + times(hits[1], ztok[source(pair, 1), :, cols])
            packs[pair, :, :, cols] = rows.astype(BF16).reshape(8, PAIR, WIDE)
        for dx in (2, 1, 3, 0):
            for dc in (0, 1):
                if dx or dc:
                    packet(pair, dx, dc).start()
        pltpu.make_async_copy(
            packs.at[pair, x * 2 + c], slots.at[pair, x * 2 + c], p_recv.at[pair]
        ).start()

    near_r = (2 * (zl % 2) + 3) % 4
    wait_bytes(ztok.at[0], t_recv.at[near_r])
    pack(0)
    spread(5)
    relay(2)
    for b in range(2):
        wait_bytes(ztok.at[0], t_recv.at[(zl + 4 - source(1, b)) % 4])
    pack(1)
    spread(6)
    relay(3)
    spread(7)

    @pl.loop(4, 8)
    def _(k):
        relay(k)

    for pair in range(2):
        wait_bytes(packs.at[pair, pl.ds(0, 7)], p_send.at[pair])
        wait_bytes(slots.at[pair], p_recv.at[pair])

    def answer(pair, dx, dc):
        to = device(x + dx, y, z, c + dc)
        return send_to(
            packs.at[pair, ((x + dx) % 4) * 2 + (c + dc) % 2], rback.at[pair, x * 2 + c],
            b_send.at[pair], b_recv.at[pair], to,
        )

    def experts(dy, first, last):
        w = ((y + dy) % 4) * 2

        def wide(which, n, count):
            return jnp.concatenate(
                [wbuf[w, which, pl.ds(n, count), :], wbuf[w + 1, which, pl.ds(n, count), :]], axis=1
            )

        @pl.loop(0, 4)
        def _(t):
            pair = 1 - t // 2
            at = pl.ds((t % 2) * 4, 4)
            rows = slots[pair, at].reshape(4 * PAIR, WIDTH)
            gate = times(rows, wide(0, 0, WIDTH))
            up = times(rows, wide(1, 0, WIDTH))
            hidden = (gate * (1.0 / (1.0 + jnp.exp(-gate))) * up).astype(BF16)
            for n in range(0, WIDTH, WIDE):
                cols = pl.ds(n, WIDE)
                got = times(hidden, wide(2, n, WIDE), ((1,), (1,))).reshape(4, PAIR, WIDE)
                if not first:
                    got = got + total[pair, at, :, cols]
                if last:
                    packs[pair, at, :, cols] = got.astype(BF16)
                else:
                    total[pair, at, :, cols] = got

    experts(0, True, False)
    experts(1, False, False)
    experts(3, False, False)
    @pl.loop(0, 8)
    def _(k):
        for way in range(2):
            passed = group(k, 2, way * half, half)
            wait_bytes(passed, r_recv.at[way, k])

    experts(2, False, True)
    for pair in (1, 0):
        for dx in (2, 1, 3, 0):
            for dc in (0, 1):
                if dx or dc:
                    answer(pair, dx, dc).start()
        pltpu.make_async_copy(
            packs.at[pair, x * 2 + c], rback.at[pair, x * 2 + c], b_recv.at[pair]
        ).start()

    def combine(pair):
        wait_bytes(rback.at[pair], b_recv.at[pair])
        for b in range(2):
            from_z = source(pair, b)
            fields = zroute[from_z]
            hit = times(fields, picker(0, True)) == spots(b, True)
            high = jnp.where(hit, times(fields, picker(1, True)), 0.0).astype(BF16)
            low = jnp.where(hit, times(fields, picker(2, True)), 0.0).astype(BF16)
            for n in range(0, WIDTH, WIDE):
                cols = pl.ds(n, WIDE)
                rows = rback[pair, :, :, cols].reshape(SLOTS, WIDE)
                c_out[from_z, :, cols] = (times(high, rows) + times(low, rows)).astype(BF16)

    def back(from_z):
        r = (from_z + 4 - zl) % 4
        return send_to(
            c_out.at[from_z], c_in.at[r], c_send.at[r], c_recv.at[r], device(x, y, zh * 4 + from_z, c)
        )

    combine(1)
    for b in range(2):
        back(source(1, b)).start()
    combine(0)
    near = zl + 1 - 2 * (zl % 2)
    back(near).start()
    result = resid[...] + c_out[zl].astype(F32)
    for r in (1, 3, 2):
        wait_bytes(c_in.at[r], c_recv.at[r])
        result = result + c_in[r].astype(F32)
    out_ref[...] = result.astype(BF16)

    wait_bytes(own_w.at[pl.ds(0, 7)], a_send.at[0])

    @pl.loop(1, 8)
    def _(k):
        wait_bytes(own_w.at[pl.ds(0, 8)], a_send.at[k])

    @pl.loop(0, 8)
    def _(k):
        for way in range(2):
            wait_bytes(group(k, 0), s_send.at[way, k])
            wait_bytes(group(k, 0, 0, half), r_send.at[way, k])

    for r in (1, 2, 3):
        y_copy(r).wait_send()
        token_copy(r).wait_send()
        route_copy(r).wait_send()
        wait_bytes(c_out.at[0], c_send.at[r])
    z_copy.wait_send()
    for pair in range(2):
        wait_bytes(packs.at[pair, pl.ds(0, 7)], b_send.at[pair])


def layer(own_w, x, own_x, attn_gain, w_qkv, w_out, cache, bias, moe_gain, route):
    dma = pltpu.SemaphoreType.DMA
    vmem = pltpu.VMEM
    return pl.pallas_call(
        layer_kernel,
        out_shape=jax.ShapeDtypeStruct((OWN, WIDTH), BF16),
        in_specs=[pl.BlockSpec(memory_space=pltpu.VMEM)] * 10,
        out_specs=pl.BlockSpec(memory_space=pltpu.VMEM),
        scratch_shapes=[
            vmem((8, 3, WIDTH, 128), BF16),
            vmem((ROWS, 6 * HD), BF16),
            vmem((ROWS, 2 * HD), BF16),
            vmem((ROWS // 4, WIDTH), F32),
            vmem((4, ROWS // 4, WIDTH), BF16),
            vmem((4, ROWS // 4, WIDTH), BF16),
            vmem((OWN, WIDTH), BF16),
            vmem((OWN, WIDTH), BF16),
            vmem((OWN, WIDTH), F32),
            vmem((4, OWN, WIDTH), BF16),
            vmem((4, OWN, 128), BF16),
            vmem((2, 8, PAIR, WIDTH), BF16),
            vmem((2, 8, PAIR, WIDTH), BF16),
            vmem((2, 8, PAIR, WIDTH), F32),
            vmem((2, 8, PAIR, WIDTH), BF16),
            vmem((4, OWN, WIDTH), BF16),
            vmem((4, OWN, WIDTH), BF16),
            dma((8,)), dma((8,)),
            dma((2, 8)), dma((2, 8)), dma((2, 8)), dma((2, 8)),
            dma((4,)), dma((4,)), dma, dma,
            dma((4,)), dma((4,)), dma((4,)), dma((4,)),
            dma((2,)), dma((2,)), dma((2,)), dma((2,)), dma((4,)), dma((4,)),
        ],
        compiler_params=pltpu.CompilerParams(
            collective_id=0, has_side_effects=True, vmem_limit_bytes=62 * 1024 * 1024
        ),
        name="layer",
    )(own_w, x, own_x, attn_gain, w_qkv, w_out, cache, bias, moe_gain, route)


def routes(chosen, probs):
    share = probs / jnp.sum(probs, axis=-1, keepdims=True)
    onehot = (chosen[:, :, None] == jnp.arange(EXPERTS, dtype=jnp.int32)).astype(F32)
    named = jnp.sum(onehot, axis=1)
    weight = jnp.sum(onehot * share[:, :, None], axis=1)
    rows = chosen.shape[0]
    earlier = (jnp.arange(rows)[:, None] > jnp.arange(rows)[None, :]).astype(BF16)
    place = jnp.dot(earlier, named.astype(BF16), preferred_element_type=F32)
    place = jnp.where(named > 0, place, -1000.0)
    high = lax.reduce_precision(weight, 8, 7)
    low = weight - high
    fields = jnp.stack([place, high, low], axis=1).reshape(rows, 3, 4, 8)
    fields = fields.transpose(2, 0, 1, 3).reshape(4, rows, 24)
    return jnp.pad(fields, ((0, 0), (0, 0), (0, 104))).astype(BF16)


def on_device(
    x_tokens, attn_gain, w_qkv, w_out, cache, cache_len, moe_gain, w_trainer, expert_ids, route_probs
):
    rows = x_tokens[0]
    own_x = lax.dynamic_slice_in_dim(rows, lax.axis_index("kv") * OWN, OWN, 0)
    live = jnp.arange(CMAX, dtype=jnp.int32)[None, :] < cache_len[:, None]
    bias = jnp.where(live, 0.0, -1e30).astype(F32)
    out = layer(
        w_trainer.astype(BF16), rows, own_x, attn_gain[None], w_qkv.reshape(WIDTH, -1), w_out, cache, bias,
        moe_gain[None], routes(expert_ids[0], route_probs[0]),
    )
    return out[None]


def solution(mesh):
    return jax.shard_map(
        on_device,
        mesh=mesh,
        in_specs=(
            P("ex", None, None),
            P(),
            P(None, None, "kv"),
            P("kv", None),
            P("ex", None, None, "kv"),
            P("ex"),
            P(),
            P(None, None, "ex", "kv"),
            P("ex", "kv", None),
            P("ex", "kv", None),
        ),
        out_specs=P("ex", "kv", None),
        check_vma=False,
    )
```

time: 924 us -> 248 us (0.27)
  waiting for transfers between devices: 514 us -> 0 us
  blocking collectives: 266 us -> 0 us
  Pallas kernels: 0 us -> 230 us
  local copies, waits for them, and re-layouts: 64.3 us -> 10.2 us
  matrix products: 34.9 us -> 0.13 us
  starting transfers between devices: 15.1 us -> 0 us
  between operations: 13.7 us -> 0.05 us
    all_to_all x2 -> x0, waiting for transfers between devices: 366 us -> none  [the longest x1 274 us: on_device(): lax.all_to_all(full_rows, 'ex', split_axis=0, concat_axis=2, tiled=True)]
    all_to_all x1 -> x0, blocking collectives: 266 us -> none  [on_device(): block = lax.all_to_all(send, 'ex', split_axis=0, concat_axis=0, tiled=True)]
    pallas_call x0 -> x1, Pallas kernels: none -> 230 us  [layer(): pl.pallas_call(layer_kernel, out_shape=jax.ShapeDtypeStruct((OWN, WIDTH),...]
    reduce_scatter x1 -> x0, waiting for transfers between devices: 132 us -> none  [on_device(): lax.psum_scatter(jnp.dot(heads_out, w_out, preferred_element_type=jnp.flo...]
    dot_general x8 -> x1, matrix products: 30.2 us -> 0.13 us  [routes(): place = jnp.dot(earlier, named.astype(BF16), preferred_element_type=F32)]
    reshape x5 -> x2, local copies, waits for them, and re-layouts: 26.1 us -> 2.93 us  [the longest x1 2.83 us: on_device(): w_qkv.reshape(WIDTH, -1)]
    all_gather x1 -> x0, waiting for transfers between devices: 16.5 us -> none  [on_device(): full_rows = lax.all_gather(trainer, 'kv', axis=3, tiled=True)]
    all_to_all x2 -> x0, starting transfers between devices: 15.1 us -> none  [the longest x1 7.96 us: on_device(): lax.all_to_all(full_rows, 'ex', split_axis=0, concat_axis=2, tiled=True)]
  transfers between devices with their start and end apart: 4 -> 0, of which waited for: 4 -> 0; matrix products, arithmetic and copies ran while one was open for 3% -> 0% of each run, Pallas kernels for 0% -> 0%
where the time goes in v2:
time: 248 us; the launch traced here: 246 us
  Pallas kernels  230 us (93%)
  local copies, waits for them, and re-layouts  10.2 us (4%)
  other arithmetic  6.2 us (2%)
    pallas_call x1, Pallas kernels, layer(): pl.pallas_call(layer_kernel, out_shape=jax.ShapeDtypeStruct((OWN, WIDTH),...  230 us

profile of v2, /device:TPU:1, one launch (start us, length us, event | category | flops | bytes accessed | tf_op | source)
XLA Modules:
  0.0 246.2 jit_solution(8491757278458420007)
XLA Ops:
  0.0 1.7 dynamic-slice_bitcast_fusion.own_x
  1.7 0.7 reduce_sum.30
  2.4 0.7 bitcast_divide_fusion
  3.1 0.7 convert_reduce_fusion
  3.8 0.1 fusion.1
  4.0 0.1 copy.23
  4.1 0.7 pad.5.route
  4.8 3.2 %copy.21 = bf16[2048,3,256]{0,2,1:T(8,128)(2,1)S(1)} copy(bf16[2048,3,256]{2,0,1:T(8,128)(2,1)} %param.12) | data formatting | bytes 6291456 | tf_op args[2]
  8.0 2.8 %copy.24.w_qkv = bf16[2048,768]{1,0:T(8,128)(2,1)} copy(bf16[2048,768]{0,1:T(8,128)(2,1)S(1)} %bitcast.20) | data formatting | bytes 6291456 | tf_op jit(solution)/shard_map/reshape | solution.py:445
  10.8 0.0 copy-start
  10.8 3.4 %convert_element_type.13.own_w = bf16[32,3,64,128]{3,2,1,0:T(8,128)(2,1)} convert(f32[32,3,64,128]{3,2,1,0:T(8,128)} %param.17) | non-fusion elementwise | flops 786432 | bytes 4718592 | tf_op jit(solution)/shard_map/convert_element_type | solution.py:445
  14.2 0.0 copy-done
  14.2 0.7 compare_select_fusion.bias
  14.9 229.6 %layer.1 = bf16[72,2048]{1,0:T(8,128)(2,1)} custom-call(bf16[32,3,64,128]{3,2,1,0:T(8,128)(2,1)} %convert_element_type.13.own_w, bf16[576,2048]{1,0:T(8,128)(2,1)} %bitcast.21, bf16[72,2048]{1,0:T(8,128)(2,1)} %dynamic-slice_bitcast_fusion.own_x, f32[1,2048]{1,0:T(1,128)} %bitcast.23, bf16[2048,768]{1,0:T(8,128)(2,1)} %copy.24.w_qkv, ...), custom_call_target="tpu_custom_call" | custom-call | tf_op jit(solution)/shard_map/layer/pallas_call | solution.py:385
  244.5 1.7 copy.27
  (2 shorter events, 0.0 us)
Async XLA Ops:
  10.8 3.4 %copy-start = (s32[2]{0:T(128)S(1)}, s32[2]{0:T(128)}, u32[]{:S(2)}) copy-start(s32[2]{0:T(128)} %param.15) | copy-start | bytes 28

commit v3 on v2

--- a/solution.py
+++ b/solution.py
@@ -62,11 +62,12 @@
 
 
 def layer_kernel(
-    own_w, x_ref, own_x, attn_gain, w_qkv, w_out, cache, bias, moe_gain, route,
+    trainer_hbm, x_hbm, attn_gain, qkv_hbm, wout_hbm, cache_hbm, bias, moe_gain, route,
     out_ref,
-    wbuf, proj, heads, part, y_out, y_in, z_out, z_in, resid, ztok, zroute, packs, slots, total, rback, c_out, c_in,
+    raw, own_w, x_ref, own_x, w_qkv, w_out, cache, wbuf, proj, heads, part, y_out, y_in, z_out, z_in, resid, ztok, zroute, packs, slots, total, rback, c_out, c_in,
     a_send, a_recv, s_send, s_recv, r_send, r_recv, y_send, y_recv, z_send, z_recv,
-    t_send, t_recv, m_send, m_recv, p_send, p_recv, b_send, b_recv, c_send, c_recv,
+    t_send, t_recv, u_send, u_recv, m_send, m_recv, p_send, p_recv, b_send, b_recv, c_send, c_recv,
+    raw_sem, in_sem,
 ):
     x, y, z, c = position()
     kv, ex = device(x, y, z, c)
@@ -74,6 +75,21 @@
     piece_rows = own_w.shape[2]
     barrier = pltpu.get_barrier_semaphore()
 
+    def raw_copy(i):
+        return pltpu.make_async_copy(trainer_hbm.at[pl.ds(i * 8, 8)], raw.at[i % 2], raw_sem.at[i % 2])
+
+    loads = [
+        pltpu.make_async_copy(x_hbm, x_ref, in_sem.at[0]),
+        pltpu.make_async_copy(qkv_hbm, w_qkv, in_sem.at[1]),
+        pltpu.make_async_copy(cache_hbm, cache, in_sem.at[2]),
+        pltpu.make_async_copy(wout_hbm, w_out, in_sem.at[3]),
+        pltpu.make_async_copy(x_hbm.at[pl.ds(pl.multiple_of(kv * OWN, 8), OWN)], own_x, in_sem.at[4]),
+    ]
+    raw_copy(0).start()
+    raw_copy(1).start()
+    for load in loads:
+        load.start()
+
     @pl.loop(0, 8)
     def _(k):
         for dx in range(4):
@@ -89,6 +105,11 @@
 
     for dy in (1, 2, 3):
         pl.semaphore_signal(barrier, inc=1, device_id=device(x, y + dy, z, c), device_id_type=MESH)
+    for i in range(4):
+        raw_copy(i).wait()
+        own_w[pl.ds(i * 8, 8)] = raw[i % 2].astype(BF16)
+        if i < 2:
+            raw_copy(i + 2).start()
     pl.semaphore_wait(barrier, 66)
 
     def route_copy(r):
@@ -142,13 +163,20 @@
             passed = group(k, 4 - dy, way * half, half)
             send_to(passed, passed, r_send.at[way, k], r_recv.at[way, k], device(x, y + dy, z, c)).start()
 
+    loads[0].wait()
+    loads[1].wait()
+
     @pl.loop(0, 2)
     def _(i):
         rows = pl.ds(pl.multiple_of(i * (ROWS // 2), ROWS // 2), ROWS // 2)
         values = x_ref[rows, :].astype(F32)
         scale = lax.rsqrt(jnp.mean(values * values, axis=-1, keepdims=True) + 1e-06)
         normed = (values * scale * attn_gain[...]).astype(BF16)
-        proj[rows, :] = times(normed, w_qkv[...]).astype(BF16)
+        for which in range(3):
+            proj[rows, pl.ds(which * 2 * HD, 2 * HD)] = times(normed, w_qkv[which]).astype(BF16)
+
+    for load in loads[2:]:
+        load.wait()
 
     spread(0)
 
@@ -205,13 +233,25 @@
     scale = lax.rsqrt(jnp.mean(sums * sums, axis=-1, keepdims=True) + 1e-06)
     ztok[zl] = (sums * scale * moe_gain[...]).astype(BF16)
 
-    def token_copy(r):
-        return send_to(
-            ztok.at[zl], ztok.at[zl], t_send.at[r], t_recv.at[r], device(x, y, zh * 4 + (zl + r) % 4, c)
-        )
-
-    for r in (1, 3, 2):
-        token_copy(r).start()
+    near = zl + 1 - 2 * (zl % 2)
+    inner = (zl + 1) % 4 // 2
+    far_inner = (2 - zl // 2)
+
+    def column(to):
+        return device(x, y, zh * 4 + to, c)
+
+    def near_copy():
+        return send_to(ztok.at[zl], ztok.at[zl], t_send.at[0], t_recv.at[0], column(near))
+
+    def far_copy():
+        return send_to(ztok.at[zl], ztok.at[zl], t_send.at[1], t_recv.at[1 + inner], column(far_inner))
+
+    def pass_on(b):
+        block = source(1, b)
+        return send_to(ztok.at[block], ztok.at[block], u_send.at[b], u_recv.at[b], column(near))
+
+    near_copy().start()
+    far_copy().start()
     own_route.wait()
     for r in (1, 2, 3):
         wait_bytes(zroute.at[0], m_recv.at[r])
@@ -254,13 +294,24 @@
             packs.at[pair, x * 2 + c], slots.at[pair, x * 2 + c], p_recv.at[pair]
         ).start()
 
-    near_r = (2 * (zl % 2) + 3) % 4
-    wait_bytes(ztok.at[0], t_recv.at[near_r])
+    wait_bytes(ztok.at[0], t_recv.at[0])
     pack(0)
+
+    @pl.when(inner == 1)
+    def _():
+        wait_bytes(ztok.at[0], t_recv.at[2])
+        pass_on(zl // 2).start()
+        wait_bytes(ztok.at[0], t_recv.at[1])
+        pass_on(1 - zl // 2).start()
+
     spread(5)
     relay(2)
-    for b in range(2):
-        wait_bytes(ztok.at[0], t_recv.at[(zl + 4 - source(1, b)) % 4])
+
+    @pl.when(inner == 0)
+    def _():
+        for b in range(2):
+            wait_bytes(ztok.at[0], u_recv.at[b])
+
     pack(1)
     spread(6)
     relay(3)
@@ -289,10 +340,8 @@
                 [wbuf[w, which, pl.ds(n, count), :], wbuf[w + 1, which, pl.ds(n, count), :]], axis=1
             )
 
-        @pl.loop(0, 4)
-        def _(t):
-            pair = 1 - t // 2
-            at = pl.ds((t % 2) * 4, 4)
+        def step(pair, t):
+            at = pl.ds(t * 4, 4)
             rows = slots[pair, at].reshape(4 * PAIR, WIDTH)
             gate = times(rows, wide(0, 0, WIDTH))
             up = times(rows, wide(1, 0, WIDTH))
@@ -307,9 +356,23 @@
                 else:
                     total[pair, at, :, cols] = got
 
+        if last:
+            for pair in (1, 0):
+                pl.loop(0, 2)(lambda t: step(pair, t))
+                for dx in (2, 1, 3, 0):
+                    for dc in (0, 1):
+                        if dx or dc:
+                            answer(pair, dx, dc).start()
+                pltpu.make_async_copy(
+                    packs.at[pair, x * 2 + c], rback.at[pair, x * 2 + c], b_recv.at[pair]
+                ).start()
+        else:
+            pl.loop(0, 4)(lambda t: step(t // 2, t % 2))
+
     experts(0, True, False)
     experts(1, False, False)
     experts(3, False, False)
+
     @pl.loop(0, 8)
     def _(k):
         for way in range(2):
@@ -317,14 +380,6 @@
             wait_bytes(passed, r_recv.at[way, k])
 
     experts(2, False, True)
-    for pair in (1, 0):
-        for dx in (2, 1, 3, 0):
-            for dc in (0, 1):
-                if dx or dc:
-                    answer(pair, dx, dc).start()
-        pltpu.make_async_copy(
-            packs.at[pair, x * 2 + c], rback.at[pair, x * 2 + c], b_recv.at[pair]
-        ).start()
 
     def combine(pair):
         wait_bytes(rback.at[pair], b_recv.at[pair])
@@ -349,7 +404,6 @@
     for b in range(2):
         back(source(1, b)).start()
     combine(0)
-    near = zl + 1 - 2 * (zl % 2)
     back(near).start()
     result = resid[...] + c_out[zl].astype(F32)
     for r in (1, 3, 2):
@@ -371,23 +425,38 @@
 
     for r in (1, 2, 3):
         y_copy(r).wait_send()
-        token_copy(r).wait_send()
         route_copy(r).wait_send()
         wait_bytes(c_out.at[0], c_send.at[r])
     z_copy.wait_send()
+    near_copy().wait_send()
+    far_copy().wait_send()
+
+    @pl.when(inner == 1)
+    def _():
+        for b in range(2):
+            pass_on(b).wait_send()
+
     for pair in range(2):
         wait_bytes(packs.at[pair, pl.ds(0, 7)], b_send.at[pair])
 
 
-def layer(own_w, x, own_x, attn_gain, w_qkv, w_out, cache, bias, moe_gain, route):
+def layer(trainer, x, attn_gain, w_qkv, w_out, cache, bias, moe_gain, route):
     dma = pltpu.SemaphoreType.DMA
     vmem = pltpu.VMEM
+    anywhere, held = pl.BlockSpec(memory_space=pl.ANY), pl.BlockSpec(memory_space=pltpu.VMEM)
     return pl.pallas_call(
         layer_kernel,
         out_shape=jax.ShapeDtypeStruct((OWN, WIDTH), BF16),
-        in_specs=[pl.BlockSpec(memory_space=pltpu.VMEM)] * 10,
-        out_specs=pl.BlockSpec(memory_space=pltpu.VMEM),
+        in_specs=[anywhere, anywhere, held, anywhere, anywhere, anywhere, held, held, held],
+        out_specs=held,
         scratch_shapes=[
+            vmem((2, 8) + trainer.shape[1:], F32),
+            vmem(trainer.shape, BF16),
+            vmem(x.shape, BF16),
+            vmem((OWN, WIDTH), BF16),
+            vmem(w_qkv.shape, BF16),
+            vmem(w_out.shape, BF16),
+            vmem(cache.shape, BF16),
             vmem((8, 3, WIDTH, 128), BF16),
             vmem((ROWS, 6 * HD), BF16),
             vmem((ROWS, 2 * HD), BF16),
@@ -408,14 +477,15 @@
             dma((8,)), dma((8,)),
             dma((2, 8)), dma((2, 8)), dma((2, 8)), dma((2, 8)),
             dma((4,)), dma((4,)), dma, dma,
-            dma((4,)), dma((4,)), dma((4,)), dma((4,)),
+            dma((2,)), dma((3,)), dma((2,)), dma((2,)), dma((4,)), dma((4,)),
             dma((2,)), dma((2,)), dma((2,)), dma((2,)), dma((4,)), dma((4,)),
+            dma((2,)), dma((5,)),
         ],
         compiler_params=pltpu.CompilerParams(
             collective_id=0, has_side_effects=True, vmem_limit_bytes=62 * 1024 * 1024
         ),
         name="layer",
-    )(own_w, x, own_x, attn_gain, w_qkv, w_out, cache, bias, moe_gain, route)
+    )(trainer, x, attn_gain, w_qkv, w_out, cache, bias, moe_gain, route)
 
 
 def routes(chosen, probs):
@@ -438,11 +508,10 @@
     x_tokens, attn_gain, w_qkv, w_out, cache, cache_len, moe_gain, w_trainer, expert_ids, route_probs
 ):
     rows = x_tokens[0]
-    own_x = lax.dynamic_slice_in_dim(rows, lax.axis_index("kv") * OWN, OWN, 0)
     live = jnp.arange(CMAX, dtype=jnp.int32)[None, :] < cache_len[:, None]
     bias = jnp.where(live, 0.0, -1e30).astype(F32)
     out = layer(
-        w_trainer.astype(BF16), rows, own_x, attn_gain[None], w_qkv.reshape(WIDTH, -1), w_out, cache, bias,
+        w_trainer, rows, attn_gain[None], w_qkv.transpose(1, 0, 2), w_out, cache, bias,
         moe_gain[None], routes(expert_ids[0], route_probs[0]),
     )
     return out[None]

time: 248 us -> 233 us (0.940)
  local copies, waits for them, and re-layouts: 10.2 us -> 2.45 us
  Pallas kernels: 230 us -> 224 us
  other arithmetic: 6.2 us -> 3.46 us
    pallas_call x1, Pallas kernels: 230 us -> 224 us  [layer(): pl.pallas_call(layer_kernel, out_shape=jax.ShapeDtypeStruct((OWN, WIDTH),...]
    convert_element_type x1 -> x0, other arithmetic: 3.39 us -> none  [on_device(): w_trainer.astype(BF16)]
    unnamed x4 -> x1, local copies, waits for them, and re-layouts: 4.9 us -> 1.69 us
    reshape x1 -> x0, local copies, waits for them, and re-layouts: 2.83 us -> none  [on_device(): w_qkv.reshape(WIDTH, -1)]
where the time goes in v3:
time: 233 us; the launch traced here: 230 us
  Pallas kernels  224 us (96%)
  other arithmetic  3.46 us (1%)
  local copies, waits for them, and re-layouts  2.45 us (1%)
    pallas_call x1, Pallas kernels, layer(): pl.pallas_call(layer_kernel, out_shape=jax.ShapeDtypeStruct((OWN, WIDTH),...  224 us

profile of v3, /device:TPU:1, one launch (start us, length us, event | category | flops | bytes accessed | tf_op | source)
XLA Modules:
  0.0 230.5 jit_solution(12047156515909385284)
XLA Ops:
  0.0 0.7 reduce_sum.30
  0.7 0.7 bitcast_divide_fusion
  1.4 1.3 compare_select_fusion.bias
  2.7 0.7 convert_reduce_fusion
  3.4 0.1 fusion.1
  3.6 0.1 copy.19
  3.7 0.7 pad.5.route
  4.4 224.4 %layer.1 = bf16[72,2048]{1,0:T(8,128)(2,1)} custom-call(f32[32,3,64,128]{3,2,1,0:T(8,128)} %trainer_hbm.1, bf16[576,2048]{1,0:T(8,128)(2,1)} %bitcast.19, f32[1,2048]{1,0:T(1,128)} %bitcast.21, bf16[3,2048,256]{2,1,0:T(8,128)(2,1)} %bitcast.18, bf16[256,2048]{1,0:T(8,128)(2,1)} %wout_hbm.1, bf16[2,2,512,256]{3,2,1,0:T(8,128)(2,1)} %cache_hbm.1, ...), custom_call_target="tpu_custom_call" | custom-call | tf_op jit(solution)/shard_map/layer/pallas_call | solution.py:447
  228.8 1.7 copy.22
  (2 shorter events, 0.0 us)
